TPU v7x, 32 devices: a whole 2x2x4 slice. The times are simulated.
32 devices in a mesh: sec: 4 (over y, x), dev: 8 (over z, core).
Axes of the slice: x: 2, y: 2, z: 4, core: 2. Of those that a mesh axis runs over, the one named last changes fastest.
Arguments:
- child_panel: bfloat16 [4, 6144, 2048], P('sec', 'dev'), may hold values from -0.23925781 to 0.23925781
- child_inverse: bfloat16 [4, 2048, 2048], P('sec'), may hold values from -0.03756505 to 1.5, as said below
- child_map: int32 [4, 48], replicated, may hold values from 0 to 63, as said below
- parent_front: bfloat16 [8192, 8192], P('sec', 'dev'), may hold values from -6 to 6
- parent_inverse: bfloat16 [1024, 1024], replicated, may hold values from -0.00166015625 to 0.046875, as said below
- parent_pivots: int32 [8], replicated, may hold values from 0 to 63, as said below
Outputs:
- parent_update: float32 [8192, 8192], P('sec', 'dev')
- parent_factor: bfloat16 [8192, 1024], P('sec')
Inputs may be any that keep to these rules, and one draw needn't show every extreme that they name: `child_map`: each row names 48 different parent blocks. `parent_pivots`: 8 different parent blocks. `child_inverse`: upper triangular with positive diagonal. `parent_inverse`: upper triangular with positive diagonal.
All inputs are finite; a program needn't handle non-finite values.
Results may differ from a plain program's by a relative error of at most 0.014.
Values may be sent and summed in bfloat16 or wider, within the bound.
A program may use at most 128 MiB of HBM per device.

v0:
```python
import jax
import jax.numpy as jnp
from jax import lax
from jax.sharding import PartitionSpec as P

BLK = 128
PORD = 8192


def spread_2(value, axis, source):
    kept = jnp.where(lax.axis_index(axis) == source, value, 0).astype(value.dtype)
    return lax.psum(kept, axis)


def outer_rows(left_rows, right_rows):
    return lax.dot_general(
        left_rows, right_rows, (((1,), (1,)), ((), ())), preferred_element_type=jnp.float32
    )


def local(child_panel, child_inverse, child_map, parent_front, parent_inverse, parent_pivots):
    dev_count = lax.axis_size("dev")
    sec_count = lax.axis_size("sec")
    sec_index = lax.axis_index("sec")
    dev_index = lax.axis_index("dev")
    block_count = PORD // BLK
    cols_dev = block_count // dev_count
    rows_sec = block_count // sec_count
    col_width = cols_dev * BLK
    my_map = lax.dynamic_index_in_dim(child_map, sec_index, 0, keepdims=False)
    child_blocks = my_map.shape[0]
    place_map = (my_map[:, None] == jnp.arange(block_count, dtype=jnp.int32)[None, :]).astype(
        jnp.bfloat16
    )
    lower_rows = jnp.dot(
        child_panel[0], child_inverse[0], preferred_element_type=jnp.float32
    ).astype(jnp.bfloat16)
    col_targets = dev_index * cols_dev + jnp.arange(cols_dev, dtype=jnp.int32)
    whole_rows = lax.all_gather(lower_rows, "dev", axis=0, tiled=True)
    pick_cols = (my_map[None, :] == col_targets[:, None]).astype(jnp.bfloat16)
    chosen = jnp.einsum(
        "mj,jbp->mbp",
        pick_cols,
        whole_rows.reshape(child_blocks, BLK, -1),
        preferred_element_type=jnp.float32,
    ).astype(jnp.bfloat16)
    by_columns = (-outer_rows(whole_rows, chosen.reshape(col_width, -1))).astype(jnp.bfloat16)
    spread = jnp.einsum(
        "jm,jbc->mbc",
        place_map,
        by_columns.reshape(child_blocks, BLK, col_width),
        preferred_element_type=jnp.float32,
    ).reshape(PORD, col_width)
    summed = lax.psum_scatter(
        spread.astype(jnp.bfloat16), "sec", scatter_dimension=0, tiled=True
    ).astype(jnp.float32)
    assembled = parent_front.astype(jnp.float32) + summed
    panel_values = assembled.astype(jnp.bfloat16)
    pivot_blocks = parent_pivots.shape[0]
    pick_pivots = (parent_pivots[None, :] == col_targets[:, None]).astype(jnp.bfloat16)
    selected = jnp.einsum(
        "mr,rbk->mbk",
        pick_pivots,
        parent_inverse.reshape(pivot_blocks, BLK, -1),
        preferred_element_type=jnp.float32,
    ).astype(jnp.bfloat16)
    partial_sum = jnp.dot(
        panel_values, selected.reshape(col_width, -1), preferred_element_type=jnp.float32
    )
    parent_factor = lax.psum(partial_sum.astype(jnp.bfloat16), "dev")
    my_blocks = sec_index * rows_sec + jnp.arange(rows_sec, dtype=jnp.int32)
    is_pivot = jnp.any(parent_pivots[None, :] == my_blocks[:, None], axis=1)
    row_pivot = jnp.repeat(is_pivot, BLK)
    trailing = jnp.where(row_pivot[:, None], jnp.zeros_like(parent_factor), parent_factor)
    offset = dev_index * cols_dev % rows_sec * BLK
    root_sec = dev_index * cols_dev // rows_sec
    column_rows = lax.dynamic_slice_in_dim(trailing, offset, col_width, 0)
    column_factor = spread_2(column_rows, "sec", root_sec)
    parent_update = assembled - outer_rows(trailing, column_factor)
    return (parent_update, parent_factor)


def solution(mesh):
    placed = (P("sec", "dev", None), P("sec", None, None), P(), P("sec", "dev"), P(), P())
    return jax.shard_map(
        local,
        mesh=mesh,
        in_specs=placed,
        out_specs=(P("sec", "dev"), P("sec", None)),
        check_vma=False,
    )
```

profile of v0, /device:TPU:0, one launch (start us, length us, event | category | flops | bytes accessed | tf_op | source)
XLA Modules:
  0.0 718.1 jit_solution(14454594119042678381)
XLA Ops:
  7.2 0.0 copy-start
  7.2 0.0 all-gather.2.cloned.1.call-start
  7.2 1.8 copy-done
  9.1 10.2 %fusion.19 = bf16[768,2048]{1,0:T(8,128)(2,1)} fusion(bf16[1,2048,2048]{2,1,0:T(8,128)(2,1)} %param.7, bf16[1,768,2048]{2,1,0:T(8,128)(2,1)S(1)} %copy-done), kind=kOutput, calls=%fused_computation.15 | convolution fusion | flops 6444023808 | bytes 14680064 | tf_op jit(solution)/shard_map/dot_general | solution.py:35
  19.2 0.0 all-gather.2.cloned.1.call-update
  19.3 0.0 reduce-scatter.2.cloned.1.call-start
  19.3 0.7 dynamic-slice_bitcast_fusion
  20.0 222.0 %all-gather.2.cloned.1.call-done = bf16[6144,2048]{1,0:T(8,128)(2,1)} async-done(((bf16[768,2048]{1,0:T(8,128)(2,1)}), bf16[6144,2048]{1,0:T(8,128)(2,1)}) %all-gather.2.cloned.1.call-update) | async-done | bytes 25165840 | tf_op jit(solution)/shard_map/all_gather | solution.py:39
  242.0 39.9 %fusion.16 = bf16[8,128,2048]{2,0,1:T(8,128)(2,1)S(1)} fusion(bf16[48,128,2048]{2,1,0:T(8,128)(2,1)} %bitcast.33, s32[48]{0:T(128)S(1)} %dynamic-slice_bitcast_fusion, s32[8]{0:T(128)S(1)} %iota_add_fusion.1), kind=kOutput, calls=%fused_computation.14 | convolution fusion | flops 203424128 | bytes 29360352 | tf_op jit(solution)/shard_map/mj,jbp->mbp/dot_general | solution.py:41
  281.9 2.3 copy.18
  284.2 31.7 %negate_convert_fusion = bf16[6144,1024]{1,0:T(8,128)(2,1)} fusion(bf16[6144,2048]{1,0:T(8,128)(2,1)} %all-gather.2.cloned.1.call-done, bf16[1024,2048]{1,0:T(8,128)(2,1)S(1)} %bitcast.35), kind=kOutput, calls=%fused_computation.2 | convolution fusion | flops 25782386688 | bytes 41943040 | tf_op jit(solution)/shard_map/dot_general | solution.py:16
  315.8 25.8 %fusion.4 = bf16[64,128,1024]{2,0,1:T(8,128)(2,1)} fusion(bf16[48,128,1024]{2,1,0:T(8,128)(2,1)} %bitcast.34, s32[48]{0:T(128)S(1)} %dynamic-slice_bitcast_fusion), kind=kOutput, calls=%fused_computation.5 | convolution fusion | flops 813698048 | bytes 29360320 | tf_op jit(solution)/shard_map/jm,jbc->mbc/dot_general | solution.py:48
  341.7 18.6 %copy.20 = bf16[64,128,1024]{2,1,0:T(8,128)(2,1)} copy(bf16[64,128,1024]{2,0,1:T(8,128)(2,1)} %fusion.4) | data formatting | bytes 33554432 | tf_op jit(solution)/shard_map/convert_element_type | solution.py:55
  360.3 0.0 copy-start.4
  360.3 0.0 reduce-scatter.2.cloned.1.call-update
  360.4 0.3 all-reduce.3.cloned.1.call-start
  360.6 0.4 copy-done.4
  361.0 2.9 fusion.25
  363.9 2.5 copy.22
  366.4 146.0 %reduce-scatter.2.cloned.1.call-done = bf16[2048,1024]{1,0:T(8,128)(2,1)} async-done(((bf16[8192,1024]{1,0:T(8,128)(2,1)}), bf16[2048,1024]{1,0:T(8,128)(2,1)}) %reduce-scatter.2.cloned.1.call-update) | async-done | bytes 4194320 | tf_op jit(solution)/shard_map/reduce_scatter | solution.py:54
  512.4 10.6 %fusion.13 = bf16[2048,1024]{1,0:T(8,128)(2,1)} fusion(bf16[1024,1024]{1,0:T(8,128)(2,1)} %bitcast.37, bf16[2048,1024]{1,0:T(8,128)(2,1)} %reduce-scatter.2.cloned.1.call-done, bf16[2048,1024]{1,0:T(8,128)(2,1)} %param.9), kind=kOutput, calls=%fused_computation.13 | convolution fusion | flops 4305453056 | bytes 14680064 | tf_op jit(solution)/shard_map/dot_general | solution.py:67
  523.0 0.0 all-reduce.3.cloned.1.call-update
  523.1 0.0 all-reduce.5.cloned.1.call-start
  523.2 0.1 compare_reduce_fusion
  523.3 0.1 broadcast_bitcast_fusion
  523.3 96.4 %all-reduce.3.cloned.1.call-done = bf16[2048,1024]{1,0:T(8,128)(2,1)} async-done(((bf16[2048,1024]{1,0:T(8,128)(2,1)}), bf16[2048,1024]{1,0:T(8,128)(2,1)}) %all-reduce.3.cloned.1.call-update) | async-done | bytes 4194320 | tf_op jit(solution)/shard_map/psum | solution.py:70
  619.7 2.5 broadcast_select_fusion
  622.2 0.0 copy-start.3
  622.2 2.0 copy-done.3
  624.2 1.8 dynamic-slice_select_fusion
  626.0 0.0 all-reduce.5.cloned.1.call-update
  626.1 69.7 %all-reduce.5.cloned.1.call-done = bf16[1024,1024]{1,0:T(8,128)(2,1)} async-done(((bf16[1024,1024]{1,0:T(8,128)(2,1)}), bf16[1024,1024]{1,0:T(8,128)(2,1)}) %all-reduce.5.cloned.1.call-update) | async-done | bytes 2097168 | tf_op jit(solution)/shard_map/psum | solution.py:12
  695.7 0.0 copy-start.2
  695.8 0.0 copy-start.1
  695.8 13.6 %fusion.9 = f32[2048,1024]{1,0:T(8,128)} fusion(bf16[2048,1024]{1,0:T(8,128)(2,1)} %reduce-scatter.2.cloned.1.call-done, bf16[2048,1024]{1,0:T(8,128)(2,1)} %param.9, bf16[2048,1024]{1,0:T(8,128)(2,1)} %copy-done.3, bf16[1024,1024]{1,0:T(8,128)(2,1)} %all-reduce.5.cloned.1.call-done), kind=kOutput, calls=%fused_computation.9 | convolution fusion | flops 4303355904 | bytes 23068672 | tf_op jit(solution)/shard_map/dot_general | solution.py:16
  709.3 0.0 copy-done.2
  709.3 2.0 copy.37
  711.3 0.0 copy-done.1
  (2 shorter events, 0.0 us)
Async XLA Ops:
  7.2 1.9 copy-start
  7.2 234.8 %all-gather.2.cloned.1.call-start = ((), (), s32[]{:S(2)}) async-start(), calls=%async_computation.1 | async-start | bytes 28311552 | tf_op jit(solution)/shard_map/all_gather | solution.py:39
  19.3 493.2 %reduce-scatter.2.cloned.1.call-start = ((), (), s32[]{:S(2)}) async-start(), calls=%async_computation.2 | async-start | bytes 20971520 | tf_op jit(solution)/shard_map/reduce_scatter | solution.py:54
  360.3 0.7 copy-start.4
  360.4 259.3 %all-reduce.3.cloned.1.call-start = ((), (), s32[]{:S(2)}) async-start(), calls=%async_computation.3 | async-start | bytes 8388608 | tf_op jit(solution)/shard_map/psum | solution.py:70
  523.1 172.7 %all-reduce.5.cloned.1.call-start = ((), (), s32[]{:S(2)}) async-start(), calls=%async_computation.4 | async-start | bytes 4194304 | tf_op jit(solution)/shard_map/psum | solution.py:12
  622.2 2.0 copy-start.3
  695.7 13.6 %copy-start.2 = (bf16[2048,1024]{1,0:T(8,128)(2,1)S(1)}, bf16[2048,1024]{1,0:T(8,128)(2,1)}, u32[]{:S(2)}) copy-start(bf16[2048,1024]{1,0:T(8,128)(2,1)} %all-reduce.3.cloned.1.call-done) | copy-start | bytes 12582916
  695.8 15.6 %copy-start.1 = (bf16[1,768,2048]{2,1,0:T(8,128)(2,1)S(1)}, bf16[1,768,2048]{2,1,0:T(8,128)(2,1)}, u32[]{:S(2)}) copy-start(bf16[1,768,2048]{2,1,0:T(8,128)(2,1)} %param.6) | copy-start | bytes 9437188
Sparse Core Ops, SparseCore 0:
  19.4 222.5 all-gather.1
  360.5 151.9 reduce-scatter.1
  523.2 96.4 all-reduce.2
  626.2 69.5 all-reduce.4
where the time goes:
time: 721 us; the launch traced here: 718 us
  waiting for transfers between devices  534 us (74%)
  matrix products  135 us (19%)
  local copies, waits for them, and re-layouts  30.4 us (4%)
  between operations  14.1 us (2%)
    all_gather x1, waiting for transfers between devices, local(): whole_rows = lax.all_gather(lower_rows, 'dev', axis=0, tiled=True)  222 us
    reduce_scatter x1, waiting for transfers between devices, local(): lax.psum_scatter(spread.astype(jnp.bfloat16), 'sec', scatter_dimension=0,...  146 us
    psum x1, waiting for transfers between devices, local(): parent_factor = lax.psum(partial_sum.astype(jnp.bfloat16), 'dev')  96.4 us
    psum x1, waiting for transfers between devices, spread_2(): return lax.psum(kept, axis)  69.7 us
    dot_general x2, matrix products, outer_rows(): lax.dot_general(left_rows, right_rows, (((1,), (1,)), ((), ())), preferre...  45.2 us
    dot_general x1, matrix products, local(): jnp.einsum('mj,jbp->mbp', pick_cols, whole_rows.reshape(child_blocks, BLK...  39.9 us
    dot_general x1, matrix products, local(): jnp.einsum('jm,jbc->mbc', place_map, by_columns.reshape(child_blocks, BLK...  25.8 us
    convert_element_type x1, local copies, waits for them, and re-layouts, local(): spread.astype(jnp.bfloat16)  18.6 us
  transfers between devices with their start and end apart: 4, of which 4 were waited for; matrix products, arithmetic and copies ran while one was open for 1% of the time, Pallas kernels for 0%

commit v1 on v0

--- a/solution.py
+++ b/solution.py
@@ -9,7 +9,7 @@
 
 def spread_2(value, axis, source):
     kept = jnp.where(lax.axis_index(axis) == source, value, 0).astype(value.dtype)
-    return lax.psum(kept, axis)
+    return jnp.sum(lax.all_gather(kept, axis_name=axis), axis=0)
 
 
 def outer_rows(left_rows, right_rows):

time: 721 us -> 747 us (1.036)
  waiting for transfers between devices: 534 us -> 552 us
  other arithmetic: 4.4 us -> 11.9 us
    all_gather x0 -> x1, waiting for transfers between devices: none -> 87.7 us  [spread_2(): return jnp.sum(lax.all_gather(kept, axis_name=axis), axis=0)]
    psum x1 -> x0, waiting for transfers between devices: 69.7 us -> none  [spread_2(): return lax.psum(kept, axis)]
where the time goes in v1:
time: 747 us; the launch traced here: 744 us
  waiting for transfers between devices  552 us (74%)
  matrix products  135 us (18%)
  local copies, waits for them, and re-layouts  30.4 us (4%)
  between operations  14.1 us (2%)
  other arithmetic  11.9 us (2%)
    all_gather x1, waiting for transfers between devices, local(): whole_rows = lax.all_gather(lower_rows, 'dev', axis=0, tiled=True)  222 us
    reduce_scatter x1, waiting for transfers between devices, local(): lax.psum_scatter(spread.astype(jnp.bfloat16), 'sec', scatter_dimension=0,...  146 us
    psum x1, waiting for transfers between devices, local(): parent_factor = lax.psum(partial_sum.astype(jnp.bfloat16), 'dev')  96.1 us
    all_gather x1, waiting for transfers between devices, spread_2(): return jnp.sum(lax.all_gather(kept, axis_name=axis), axis=0)  87.7 us
    dot_general x2, matrix products, outer_rows(): lax.dot_general(left_rows, right_rows, (((1,), (1,)), ((), ())), preferre...  45.2 us
    dot_general x1, matrix products, local(): jnp.einsum('mj,jbp->mbp', pick_cols, whole_rows.reshape(child_blocks, BLK...  39.9 us
    dot_general x1, matrix products, local(): jnp.einsum('jm,jbc->mbc', place_map, by_columns.reshape(child_blocks, BLK...  25.8 us
    convert_element_type x1, local copies, waits for them, and re-layouts, local(): spread.astype(jnp.bfloat16)  18.6 us
  transfers between devices with their start and end apart: 4, of which 4 were waited for; matrix products, arithmetic and copies ran while one was open for 1% of the time, Pallas kernels for 0%

profile of v1, /device:TPU:0, one launch (start us, length us, event | category | flops | bytes accessed | tf_op | source)
XLA Modules:
  0.0 743.6 jit_solution(17383165399425119231)
XLA Ops:
  7.2 0.0 copy-start
  7.2 0.0 all-gather.4.cloned.1.call-start
  7.2 1.8 copy-done
  9.1 10.2 %fusion.19 = bf16[768,2048]{1,0:T(8,128)(2,1)} fusion(bf16[1,2048,2048]{2,1,0:T(8,128)(2,1)} %param.7, bf16[1,768,2048]{2,1,0:T(8,128)(2,1)S(1)} %copy-done), kind=kOutput, calls=%fused_computation.15 | convolution fusion | flops 6444023808 | bytes 14680064 | tf_op jit(solution)/shard_map/dot_general | solution.py:35
  19.2 0.0 all-gather.4.cloned.1.call-update
  19.3 0.0 reduce-scatter.2.cloned.1.call-start
  19.3 0.7 dynamic-slice_bitcast_fusion
  20.0 222.0 %all-gather.4.cloned.1.call-done = bf16[6144,2048]{1,0:T(8,128)(2,1)} async-done(((bf16[768,2048]{1,0:T(8,128)(2,1)}), bf16[6144,2048]{1,0:T(8,128)(2,1)}) %all-gather.4.cloned.1.call-update) | async-done | bytes 25165840 | tf_op jit(solution)/shard_map/all_gather | solution.py:39
  242.0 39.9 %fusion.16 = bf16[8,128,2048]{2,0,1:T(8,128)(2,1)S(1)} fusion(bf16[48,128,2048]{2,1,0:T(8,128)(2,1)} %bitcast.34, s32[48]{0:T(128)S(1)} %dynamic-slice_bitcast_fusion, s32[8]{0:T(128)S(1)} %iota_add_fusion.1), kind=kOutput, calls=%fused_computation.14 | convolution fusion | flops 203424128 | bytes 29360352 | tf_op jit(solution)/shard_map/mj,jbp->mbp/dot_general | solution.py:41
  281.9 2.3 copy.18
  284.2 31.7 %negate_convert_fusion = bf16[6144,1024]{1,0:T(8,128)(2,1)} fusion(bf16[6144,2048]{1,0:T(8,128)(2,1)} %all-gather.4.cloned.1.call-done, bf16[1024,2048]{1,0:T(8,128)(2,1)S(1)} %bitcast.37), kind=kOutput, calls=%fused_computation.2 | convolution fusion | flops 25782386688 | bytes 41943040 | tf_op jit(solution)/shard_map/dot_general | solution.py:16
  315.9 25.8 %fusion.4 = bf16[64,128,1024]{2,0,1:T(8,128)(2,1)} fusion(bf16[48,128,1024]{2,1,0:T(8,128)(2,1)} %bitcast.35, s32[48]{0:T(128)S(1)} %dynamic-slice_bitcast_fusion), kind=kOutput, calls=%fused_computation.5 | convolution fusion | flops 813698048 | bytes 29360320 | tf_op jit(solution)/shard_map/jm,jbc->mbc/dot_general | solution.py:48
  341.7 18.6 %copy.20 = bf16[64,128,1024]{2,1,0:T(8,128)(2,1)} copy(bf16[64,128,1024]{2,0,1:T(8,128)(2,1)} %fusion.4) | data formatting | bytes 33554432 | tf_op jit(solution)/shard_map/convert_element_type | solution.py:55
  360.3 0.0 copy-start.4
  360.3 0.0 reduce-scatter.2.cloned.1.call-update
  360.4 0.3 all-reduce.2.cloned.1.call-start
  360.6 0.4 copy-done.4
  361.0 2.9 fusion.25
  363.9 2.5 copy.22
  366.4 146.0 %reduce-scatter.2.cloned.1.call-done = bf16[2048,1024]{1,0:T(8,128)(2,1)} async-done(((bf16[8192,1024]{1,0:T(8,128)(2,1)}), bf16[2048,1024]{1,0:T(8,128)(2,1)}) %reduce-scatter.2.cloned.1.call-update) | async-done | bytes 4194320 | tf_op jit(solution)/shard_map/reduce_scatter | solution.py:54
  512.4 10.6 %fusion.13 = bf16[2048,1024]{1,0:T(8,128)(2,1)} fusion(bf16[1024,1024]{1,0:T(8,128)(2,1)} %bitcast.39, bf16[2048,1024]{1,0:T(8,128)(2,1)} %reduce-scatter.2.cloned.1.call-done, bf16[2048,1024]{1,0:T(8,128)(2,1)} %param.9), kind=kOutput, calls=%fused_computation.13 | convolution fusion | flops 4305453056 | bytes 14680064 | tf_op jit(solution)/shard_map/dot_general | solution.py:67
  523.0 0.0 all-reduce.2.cloned.1.call-update
  523.1 0.3 all-gather.6.cloned.1.call-start
  523.4 0.1 compare_reduce_fusion
  523.5 0.1 broadcast_bitcast_fusion
  523.6 96.1 %all-reduce.2.cloned.1.call-done = bf16[2048,1024]{1,0:T(8,128)(2,1)} async-done(((bf16[2048,1024]{1,0:T(8,128)(2,1)}), bf16[2048,1024]{1,0:T(8,128)(2,1)}) %all-reduce.2.cloned.1.call-update) | async-done | bytes 4194320 | tf_op jit(solution)/shard_map/psum | solution.py:70
  619.7 2.5 broadcast_select_fusion
  622.2 0.0 copy-start.3
  622.2 2.0 copy-done.3
  624.2 1.8 dynamic-slice_select_fusion
  626.0 0.0 all-gather.6.cloned.1.call-update
  626.1 87.7 %all-gather.6.cloned.1.call-done = bf16[4096,1024]{1,0:T(8,128)(2,1)} async-done(((bf16[1024,1024]{1,0:T(8,128)(2,1)}), bf16[4096,1024]{1,0:T(8,128)(2,1)}) %all-gather.6.cloned.1.call-update) | async-done | bytes 8388624 | tf_op jit(solution)/shard_map/all_gather | solution.py:12
  713.7 7.5 %reduce_sum.12 = bf16[1024,1024]{1,0:T(8,128)(2,1)} reduce(bf16[4,1024,1024]{2,1,0:T(8,128)(2,1)} %bitcast.36, bf16[]{:T(256)} %constant.46.clone.1), dimensions={0}, to_apply=%region_3.4 | reduce | flops 3145728 | bytes 10485762 | tf_op jit(solution)/shard_map/reduce_sum | solution.py:12
  721.2 0.0 copy-start.2
  721.2 0.0 copy-start.1
  721.2 13.6 %fusion.9 = f32[2048,1024]{1,0:T(8,128)} fusion(bf16[2048,1024]{1,0:T(8,128)(2,1)} %reduce-scatter.2.cloned.1.call-done, bf16[2048,1024]{1,0:T(8,128)(2,1)} %param.9, bf16[2048,1024]{1,0:T(8,128)(2,1)} %copy-done.3, bf16[1024,1024]{1,0:T(8,128)(2,1)} %reduce_sum.12), kind=kOutput, calls=%fused_computation.9 | convolution fusion | flops 4303355904 | bytes 23068672 | tf_op jit(solution)/shard_map/dot_general | solution.py:16
  734.8 0.0 copy-done.2
  734.8 2.0 copy.36
  736.8 0.0 copy-done.1
  (2 shorter events, 0.0 us)
Async XLA Ops:
  7.2 1.9 copy-start
  7.2 234.8 %all-gather.4.cloned.1.call-start = ((), (), s32[]{:S(2)}) async-start(), calls=%async_computation.1 | async-start | bytes 28311552 | tf_op jit(solution)/shard_map/all_gather | solution.py:39
  19.3 493.2 %reduce-scatter.2.cloned.1.call-start = ((), (), s32[]{:S(2)}) async-start(), calls=%async_computation.2 | async-start | bytes 20971520 | tf_op jit(solution)/shard_map/reduce_scatter | solution.py:54
  360.3 0.7 copy-start.4
  360.4 259.3 %all-reduce.2.cloned.1.call-start = ((), (), s32[]{:S(2)}) async-start(), calls=%async_computation.3 | async-start | bytes 8388608 | tf_op jit(solution)/shard_map/psum | solution.py:70
  523.1 190.7 %all-gather.6.cloned.1.call-start = ((), (), s32[]{:S(2)}) async-start(), calls=%async_computation.4 | async-start | bytes 10485760 | tf_op jit(solution)/shard_map/all_gather | solution.py:12
  622.2 2.0 copy-start.3
  721.2 13.6 %copy-start.2 = (bf16[2048,1024]{1,0:T(8,128)(2,1)S(1)}, bf16[2048,1024]{1,0:T(8,128)(2,1)}, u32[]{:S(2)}) copy-start(bf16[2048,1024]{1,0:T(8,128)(2,1)} %all-reduce.2.cloned.1.call-done) | copy-start | bytes 12582916
  721.2 15.6 %copy-start.1 = (bf16[1,768,2048]{2,1,0:T(8,128)(2,1)S(1)}, bf16[1,768,2048]{2,1,0:T(8,128)(2,1)}, u32[]{:S(2)}) copy-start(bf16[1,768,2048]{2,1,0:T(8,128)(2,1)} %param.6) | copy-start | bytes 9437188
Sparse Core Ops, SparseCore 0:
  19.4 222.5 all-gather.3
  360.5 151.8 reduce-scatter.1
  523.2 96.4 all-reduce.1
  626.2 87.5 all-gather.5
